TPU v7x, 512 devices: a whole 4x8x8 slice. The times are simulated.
512 devices in a mesh: tok: 8 (over z), row: 8 (over y_hi, core), col: 8 (over x, y_lo).
Axes of the slice: x: 4, y: 8 (y_hi: 4, y_lo: 2; y = y_hi * 2 + y_lo), z: 8, core: 2. Of those that a mesh axis runs over, the one named last changes fastest.
Arguments:
- activations: bfloat16 [2048, 8192], P('tok', 'row'), may hold values from -8 to 8
- gradients: bfloat16 [2048, 8192], P('tok', 'col'), may hold values from -8 to 8
- act_basis: bfloat16 [8192, 8192], P('row', ('tok', 'col')), may hold values from -1 to 1
- grad_basis: bfloat16 [8192, 8192], P('col', 'row'), may hold values from -1 to 1
- eigen_noise: float32 [8192, 8192], P('row', ('tok', 'col')), may hold values from -6 to 6
Outputs:
- scales: float32 [8192, 8192], P('row', ('tok', 'col'))
- output_shift: bfloat16 [2048, 8192], P('tok', 'col')
All inputs are finite; a program needn't handle non-finite values.
Results may differ from a plain program's by a relative error of at most 0.0064.
Values may be sent and summed in bfloat16 or wider, within the bound.
No kernel may reach another device: no remote copies, remote signals or barrier semaphores. Data moves between devices by JAX's collectives and lax.ppermute only.
A program may use at most 64 MiB of HBM per device.

v0:
```python
import jax
import jax.numpy as jnp
from jax import lax
from jax.sharding import PartitionSpec as P

damping = 0.1


def contract(former, latter, former_dim, latter_dim):
    return lax.dot_general(
        former,
        latter,
        (((former_dim,), (latter_dim,)), ((), ())),
        preferred_element_type=jnp.float32,
    )


def over_rows(summands):
    return lax.psum(summands, "row")


def over_cols(summands):
    return lax.psum(summands, "col")


def shards(activations, gradients, act_basis, grad_basis, eigen_noise):
    token_count = activations.shape[0] * lax.axis_size("tok")
    basis_cols = lax.all_gather(act_basis, "tok", axis=1, tiled=True)
    act_proj = over_rows(contract(activations, basis_cols, 1, 0))
    grad_proj = over_cols(contract(gradients, grad_basis, 1, 0))
    act_sq = (act_proj * act_proj).astype(jnp.bfloat16)
    grad_sq = (grad_proj * grad_proj).astype(jnp.bfloat16)
    summed = lax.psum_scatter(
        contract(grad_sq, act_sq, 0, 0), "tok", scatter_dimension=1, tiled=True
    )
    scales = summed / token_count
    scaled = (eigen_noise * lax.rsqrt(token_count * (scales + damping))).astype(jnp.bfloat16)
    widened = lax.all_gather(scaled, "tok", axis=1, tiled=True)
    act_half = act_proj.astype(jnp.bfloat16)
    hidden = over_cols(contract(act_half, widened, 1, 1)).astype(jnp.bfloat16)
    output_shift = over_rows(contract(hidden, grad_basis, 1, 1)).astype(jnp.bfloat16)
    return (scales, output_shift)


def solution(mesh):
    in_specs = (
        P("tok", "row"),
        P("tok", "col"),
        P("row", ("tok", "col")),
        P("col", "row"),
        P("row", ("tok", "col")),
    )
    out_specs = (P("row", ("tok", "col")), P("tok", "col"))
    return jax.shard_map(shards, mesh=mesh, in_specs=in_specs, out_specs=out_specs, check_vma=False)
```

profile of v0, /device:TPU:17, one launch (start us, length us, event | category | flops | bytes accessed | tf_op | source)
XLA Modules:
  0.0 457.0 jit_solution(1851305855588722828)
XLA Ops:
  8.0 0.0 copy-start
  8.0 0.0 all-gather.3.cloned.1.call-start
  8.1 0.7 all-gather.3.cloned.1.call-update
  8.7 0.0 copy-start.1
  8.8 0.0 all-reduce.5.cloned.1.call-start
  8.8 0.8 copy-done
  9.6 2.7 fusion.5
  12.3 0.0 all-reduce.5.cloned.1.call-update
  12.4 0.0 all-reduce.7.cloned.1.call-start
  12.4 49.3 %all-gather.3.cloned.1.call-done = bf16[1024,1024]{1,0:T(8,128)(2,1)} async-done(((bf16[1024,128]{1,0:T(8,128)(2,1)}), bf16[1024,1024]{1,0:T(8,128)(2,1)}) %all-gather.3.cloned.1.call-update) | async-done | bytes 2097168 | tf_op jit(solution)/shard_map/all_gather | solution.py:28
  61.7 0.0 copy-done.1
  61.7 3.3 fusion.6
  65.0 0.0 all-reduce.7.cloned.1.call-update
  65.0 0.0 reduce-scatter.2.cloned.1.call-start
  65.0 38.5 %all-reduce.5.cloned.1.call-done = f32[256,1024]{1,0:T(8,128)} async-done(((f32[256,1024]{1,0:T(8,128)}), f32[256,1024]{1,0:T(8,128)}) %all-reduce.5.cloned.1.call-update) | async-done | bytes 1048592 | tf_op jit(solution)/shard_map/psum | solution.py:23
  103.5 89.2 %all-reduce.7.cloned.1.call-done = f32[256,1024]{1,0:T(8,128)} async-done(((f32[256,1024]{1,0:T(8,128)}), f32[256,1024]{1,0:T(8,128)}) %all-reduce.7.cloned.1.call-update) | async-done | bytes 1048592 | tf_op jit(solution)/shard_map/psum | solution.py:19
  192.7 4.2 fusion
  196.9 0.0 copy-start.2
  196.9 0.0 reduce-scatter.2.cloned.1.call-update
  196.9 0.0 all-gather.5.cloned.1.call-start
  197.0 57.3 %reduce-scatter.2.cloned.1.call-done = f32[1024,128]{1,0:T(8,128)} async-done(((f32[1024,1024]{1,0:T(8,128)}), f32[1024,128]{1,0:T(8,128)}) %reduce-scatter.2.cloned.1.call-update) | async-done | bytes 524304 | tf_op jit(solution)/shard_map/reduce_scatter | solution.py:33
  254.3 0.0 copy-done.2
  254.3 2.0 multiply_convert_fusion.4
  256.3 0.0 all-gather.5.cloned.1.call-update
  256.3 44.6 %all-gather.5.cloned.1.call-done = bf16[1024,1024]{1,0:T(8,128)(2,1)} async-done(((bf16[1024,128]{1,0:T(8,128)(2,1)}), bf16[1024,1024]{1,0:T(8,128)(2,1)}) %all-gather.5.cloned.1.call-update) | async-done | bytes 2097168 | tf_op jit(solution)/shard_map/all_gather | solution.py:38
  300.9 2.7 fusion.3
  303.6 64.5 %all-reduce.8 = bf16[256,1024]{1,0:T(8,128)(2,1)} all-reduce(f32[256,1024]{1,0:T(8,128)S(1)} %fusion.3), channel_id=1, replica_groups=mesh['tok'=8,'row'=8,'col'=8] {'col'}, use_global_device_ids=true, to_apply=%region_3.0 | all-reduce | flops 262144 | bytes 1572864 | tf_op jit(solution)/shard_map/psum | solution.py:23
  368.1 1.8 fusion.7
  369.8 80.0 %all-reduce.9 = bf16[256,1024]{1,0:T(8,128)(2,1)} all-reduce(f32[256,1024]{1,0:T(8,128)S(1)} %fusion.7), channel_id=1, replica_groups=mesh['tok'=8,'row'=8,'col'=8] {'row'}, use_global_device_ids=true, to_apply=%region_4.0 | all-reduce | flops 262144 | bytes 1572864 | tf_op jit(solution)/shard_map/psum | solution.py:19
Async XLA Ops:
  8.0 1.6 copy-start
  8.0 53.7 %all-gather.3.cloned.1.call-start = ((), (), s32[]{:S(2)}) async-start(), calls=%async_computation.2 | async-start | bytes 2359296 | tf_op jit(solution)/shard_map/all_gather | solution.py:28
  8.7 52.9 %copy-start.1 = (bf16[256,1024]{1,0:T(8,128)(2,1)S(1)}, bf16[256,1024]{1,0:T(8,128)(2,1)}, u32[]{:S(2)}) copy-start(bf16[256,1024]{1,0:T(8,128)(2,1)} %param.5) | copy-start | bytes 1572868
  8.8 94.8 %all-reduce.5.cloned.1.call-start = ((), (), s32[]{:S(2)}) async-start(), calls=%async_computation.1 | async-start | bytes 2097152 | tf_op jit(solution)/shard_map/psum | solution.py:23
  12.4 180.3 %all-reduce.7.cloned.1.call-start = ((), (), s32[]{:S(2)}) async-start(), calls=%async_computation.3 | async-start | bytes 2097152 | tf_op jit(solution)/shard_map/psum | solution.py:19
  65.0 189.3 %reduce-scatter.2.cloned.1.call-start = ((), (), s32[]{:S(2)}) async-start(), calls=%async_computation.4 | async-start | bytes 4718592 | tf_op jit(solution)/shard_map/reduce_scatter | solution.py:33
  196.9 57.4 %copy-start.2 = (f32[1024,128]{1,0:T(8,128)S(1)}, f32[1024,128]{1,0:T(8,128)}, u32[]{:S(2)}) copy-start(f32[1024,128]{1,0:T(8,128)} %param.9) | copy-start | bytes 1572868
  196.9 104.0 %all-gather.5.cloned.1.call-start = ((), (), s32[]{:S(2)}) async-start(), calls=%async_computation.5 | async-start | bytes 2359296 | tf_op jit(solution)/shard_map/all_gather | solution.py:38
Sparse Core Ops, SparseCore 0:
  10.8 50.8 all-gather.2
  197.1 57.1 reduce-scatter.1
  256.9 44.0 all-gather.4
Sparse Core Ops, SparseCore 1:
  12.4 91.0 all-reduce.4
  106.3 86.3 all-reduce.6
where the time goes:
time: 457 us
  waiting for transfers between devices  280 us (61%)
  blocking collectives  145 us (32%)
  between operations  15.2 us (3%)
  matrix products  14.7 us (3%)
    psum x1, waiting for transfers between devices, over_rows(): return lax.psum(summands, 'row')  89.2 us
    psum x1, blocking collectives, over_rows(): return lax.psum(summands, 'row')  80 us
    psum x1, blocking collectives, over_cols(): return lax.psum(summands, 'col')  64.5 us
    reduce_scatter x1, waiting for transfers between devices, shards(): lax.psum_scatter(contract(grad_sq, act_sq, 0, 0), 'tok', scatter_dimensio...  57.3 us
    all_gather x1, waiting for transfers between devices, shards(): basis_cols = lax.all_gather(act_basis, 'tok', axis=1, tiled=True)  49.3 us
    all_gather x1, waiting for transfers between devices, shards(): widened = lax.all_gather(scaled, 'tok', axis=1, tiled=True)  44.6 us
    psum x1, waiting for transfers between devices, over_cols(): return lax.psum(summands, 'col')  38.5 us
    dot_general x5, matrix products, contract(): lax.dot_general(former, latter, (((former_dim,), (latter_dim,)), ((), ())...  14.7 us
  transfers between devices with their start and end apart: 5, of which 5 were waited for; matrix products, arithmetic and copies ran while one was open for 1% of the time, Pallas kernels for 0%

commit v1 on v0

--- a/solution.py
+++ b/solution.py
@@ -2,6 +2,7 @@
 import jax.numpy as jnp
 from jax import lax
 from jax.sharding import PartitionSpec as P
+from jax.lax import all_gather
 
 damping = 0.1
 
@@ -20,7 +21,11 @@
 
 
 def over_cols(summands):
-    return lax.psum(summands, "col")
+
+    def _take_series(v0):
+        return all_gather(v0, axis_name="col").sum(axis=0)
+
+    return _take_series(summands)
 
 
 def shards(activations, gradients, act_basis, grad_basis, eigen_noise):

time: 457 us -> 693 us (1.52)
  the two profiles are of different devices: /device:TPU:17 before, /device:TPU:25 now
where the time goes in v1:
time: 693 us; the launch traced here: 692 us
  waiting for transfers between devices  586 us (85%)
  blocking collectives  64.4 us (9%)
  matrix products  15.1 us (2%)
  between operations  14.1 us (2%)
  other arithmetic  11.8 us (2%)
    all_gather x2, waiting for transfers between devices, _take_series(): return all_gather(v0, axis_name='col').sum(axis=0)  352 us
    psum x1, waiting for transfers between devices, over_rows(): return lax.psum(summands, 'row')  82.2 us
    psum x1, blocking collectives, over_rows(): return lax.psum(summands, 'row')  64.4 us
    reduce_scatter x1, waiting for transfers between devices, shards(): lax.psum_scatter(contract(grad_sq, act_sq, 0, 0), 'tok', scatter_dimensio...  58 us
    all_gather x1, waiting for transfers between devices, shards(): basis_cols = lax.all_gather(act_basis, 'tok', axis=1, tiled=True)  48.7 us
    all_gather x1, waiting for transfers between devices, shards(): widened = lax.all_gather(scaled, 'tok', axis=1, tiled=True)  44.3 us
    dot_general x5, matrix products, contract(): lax.dot_general(former, latter, (((former_dim,), (latter_dim,)), ((), ())...  15.1 us
  transfers between devices with their start and end apart: 6, of which 6 were waited for; matrix products, arithmetic and copies ran while one was open for 2% of the time, Pallas kernels for 0%

profile of v1, /device:TPU:25, one launch (start us, length us, event | category | flops | bytes accessed | tf_op | source)
XLA Modules:
  0.0 692.5 jit_solution(17158341057360950852)
XLA Ops:
  7.2 0.0 copy-start
  7.2 0.0 all-gather.7.cloned.1.call-start
  7.2 0.7 all-gather.7.cloned.1.call-update
  7.9 0.0 copy-start.2
  7.9 0.0 all-gather.11.cloned.1.call-start
  8.0 0.8 copy-done
  8.8 2.7 fusion.5
  11.5 0.0 all-gather.11.cloned.1.call-update
  11.5 0.0 all-reduce.3.cloned.1.call-start
  11.6 48.7 %all-gather.7.cloned.1.call-done = bf16[1024,1024]{1,0:T(8,128)(2,1)} async-done(((bf16[1024,128]{1,0:T(8,128)(2,1)}), bf16[1024,1024]{1,0:T(8,128)(2,1)}) %all-gather.7.cloned.1.call-update) | async-done | bytes 2097168 | tf_op jit(solution)/shard_map/all_gather | solution.py:33
  60.3 0.0 copy-done.2
  60.3 3.3 fusion.6
  63.6 0.0 all-reduce.3.cloned.1.call-update
  63.6 0.0 reduce-scatter.2.cloned.1.call-start
  63.7 175.3 %all-gather.11.cloned.1.call-done = f32[2048,1024]{1,0:T(8,128)} async-done(((f32[256,1024]{1,0:T(8,128)}), f32[2048,1024]{1,0:T(8,128)}) %all-gather.11.cloned.1.call-update) | async-done | bytes 8388624 | tf_op jit(solution)/shard_map/all_gather | solution.py:26
  239.0 4.4 reduce_sum.18
  243.4 82.2 %all-reduce.3.cloned.1.call-done = f32[256,1024]{1,0:T(8,128)} async-done(((f32[256,1024]{1,0:T(8,128)}), f32[256,1024]{1,0:T(8,128)}) %all-reduce.3.cloned.1.call-update) | async-done | bytes 1048592 | tf_op jit(solution)/shard_map/psum | solution.py:20
  325.6 3.9 fusion
  329.5 0.0 reduce-scatter.2.cloned.1.call-update
  329.5 0.0 copy-start.1
  329.5 0.0 all-gather.9.cloned.1.call-start
  329.6 58.0 %reduce-scatter.2.cloned.1.call-done = f32[1024,128]{1,0:T(8,128)} async-done(((f32[1024,1024]{1,0:T(8,128)}), f32[1024,128]{1,0:T(8,128)}) %reduce-scatter.2.cloned.1.call-update) | async-done | bytes 524304 | tf_op jit(solution)/shard_map/reduce_scatter | solution.py:38
  387.6 2.2 multiply_convert_fusion.4
  389.7 0.0 all-gather.9.cloned.1.call-update
  389.8 0.0 all-gather.13.cloned.1.call-start
  389.8 44.3 %all-gather.9.cloned.1.call-done = bf16[1024,1024]{1,0:T(8,128)(2,1)} async-done(((bf16[1024,128]{1,0:T(8,128)(2,1)}), bf16[1024,1024]{1,0:T(8,128)(2,1)}) %all-gather.9.cloned.1.call-update) | async-done | bytes 2097168 | tf_op jit(solution)/shard_map/all_gather | solution.py:43
  434.1 0.0 copy-done.1
  434.1 3.4 fusion.3
  437.5 0.0 all-gather.13.cloned.1.call-update
  437.5 176.7 %all-gather.13.cloned.1.call-done = f32[2048,1024]{1,0:T(8,128)} async-done(((f32[256,1024]{1,0:T(8,128)}), f32[2048,1024]{1,0:T(8,128)}) %all-gather.13.cloned.1.call-update) | async-done | bytes 8388624 | tf_op jit(solution)/shard_map/all_gather | solution.py:26
  614.2 5.2 reduce_sum.19
  619.4 1.8 fusion.7
  621.2 64.4 %all-reduce.4 = bf16[256,1024]{1,0:T(8,128)(2,1)} all-reduce(f32[256,1024]{1,0:T(8,128)S(1)} %fusion.7), channel_id=1, replica_groups=mesh['tok'=8,'row'=8,'col'=8] {'row'}, use_global_device_ids=true, to_apply=%region_4.0 | all-reduce | flops 262144 | bytes 1572864 | tf_op jit(solution)/shard_map/psum | solution.py:20
Async XLA Ops:
  7.2 1.6 copy-start
  7.2 53.1 %all-gather.7.cloned.1.call-start = ((), (), s32[]{:S(2)}) async-start(), calls=%async_computation.1 | async-start | bytes 2359296 | tf_op jit(solution)/shard_map/all_gather | solution.py:33
  7.9 52.4 %copy-start.2 = (bf16[256,1024]{1,0:T(8,128)(2,1)S(1)}, bf16[256,1024]{1,0:T(8,128)(2,1)}, u32[]{:S(2)}) copy-start(bf16[256,1024]{1,0:T(8,128)(2,1)} %param.5) | copy-start | bytes 1572868
  7.9 231.1 %all-gather.11.cloned.1.call-start = ((), (), s32[]{:S(2)}) async-start(), calls=%async_computation.5 | async-start | bytes 9437184 | tf_op jit(solution)/shard_map/all_gather | solution.py:26
  11.5 314.0 %all-reduce.3.cloned.1.call-start = ((), (), s32[]{:S(2)}) async-start(), calls=%async_computation.2 | async-start | bytes 2097152 | tf_op jit(solution)/shard_map/psum | solution.py:20
  63.6 323.9 %reduce-scatter.2.cloned.1.call-start = ((), (), s32[]{:S(2)}) async-start(), calls=%async_computation.3 | async-start | bytes 4718592 | tf_op jit(solution)/shard_map/reduce_scatter | solution.py:38
  329.5 104.6 %copy-start.1 = (f32[256,1024]{1,0:T(8,128)S(1)}, f32[256,1024]{1,0:T(8,128)}, u32[]{:S(2)}) copy-start(f32[256,1024]{1,0:T(8,128)} %all-reduce.3.cloned.1.call-done) | copy-start | bytes 3145732
  329.5 104.6 %all-gather.9.cloned.1.call-start = ((), (), s32[]{:S(2)}) async-start(), calls=%async_computation.4 | async-start | bytes 2359296 | tf_op jit(solution)/shard_map/all_gather | solution.py:43
  389.8 224.5 %all-gather.13.cloned.1.call-start = ((), (), s32[]{:S(2)}) async-start(), calls=%async_computation.6 | async-start | bytes 9437184 | tf_op jit(solution)/shard_map/all_gather | solution.py:26
Sparse Core Ops, SparseCore 0:
  10.0 50.2 all-gather.6
  62.4 176.5 all-gather.10
  241.9 83.5 all-reduce.2
  329.6 57.9 reduce-scatter.1
  390.0 44.0 all-gather.8
  437.6 176.5 all-gather.12
